TPU v7x, 256 devices: a whole 4x4x8 slice. The times are simulated.
256 devices in a mesh: gx: 16 (over x, y), gy: 16 (over z, core).
Axes of the slice: x: 4, y: 4, z: 8, core: 2. Of those that a mesh axis runs over, the one named last changes fastest.
Arguments:
- permeability: float32 [1, 16, 128, 2048], P(None, None, 'gx', 'gy'), may hold values from 0.2 to 5
- saturation: float32 [1, 16, 128, 2048], P(None, None, 'gx', 'gy'), may hold values from 0.1 to 0.9
- pressure_old: float32 [1, 16, 128, 2048], P(None, None, 'gx', 'gy'), may hold values from -6 to 6
- source: float32 [16, 128, 2048], P(None, 'gx', 'gy'), may hold values from -25 to 25
Outputs:
- pressure: float32 [1, 16, 128, 2048], P(None, None, 'gx', 'gy')
- saturation_new: float32 [1, 16, 128, 2048], P(None, None, 'gx', 'gy')
All inputs are finite; a program needn't handle non-finite values.
Results may differ from a plain program's by a relative error of at most 0.0003.
Values sent between devices are 32-bit elements; how exact they have to be, the bound alone decides.
No kernel may reach another device: no remote copies, remote signals or barrier semaphores. Data moves between devices by JAX's collectives and lax.ppermute only.
A program may use at most 64 MiB of HBM per device.

v0:
```python
import jax
import jax.numpy as jnp
from jax import lax
from jax.experimental import pallas as pl
from jax.experimental.pallas import tpu as pltpu
from jax.sharding import PartitionSpec as P


storage_term = 0.5
vertical_ratio = 0.1
step_ratio = 0.05
water_viscosity = 1.0
oil_viscosity = 2.0

NZ, ROWS, LANES, HALO = 16, 8, 128, 4
SPAN = 2 * ROWS
SEG = 16
TILES = NZ * SEG // LANES
PER = LANES // SEG
F32 = jnp.float32


def lanes(shape=(ROWS, LANES)):
    return lax.broadcasted_iota(jnp.int32, shape, len(shape) - 1)


def sublanes(shape=(ROWS, LANES)):
    return lax.broadcasted_iota(jnp.int32, shape, len(shape) - 2)


def turn(x, by, axis):
    n = x.shape[axis]
    if isinstance(by, int):
        by %= n
        if by == 0:
            return x
    return pltpu.roll(x, by, axis)


def total_mobility(s):
    return s * s / water_viscosity + (1.0 - s) * (1.0 - s) / oil_viscosity


def water_fraction(s):
    return s * s / water_viscosity / total_mobility(s)


def coefficient(ka, kb, ma, mb):
    return ka * kb * (ma + mb) / jnp.maximum(ka + kb, 1e-30)


def row_next(x):
    return turn(x, -1, 0)


def row_prev(x):
    return turn(x, 1, 0)


def col_next(x):
    return turn(x, -1, 1)


def col_prev(x):
    return turn(x, 1, 1)


def pack_columns(k_in, s_in, p_in, q_in, to_prev, to_next, k, s, p, q, sems):
    copies = [pltpu.make_async_copy(a, b, sems.at[i]) for i, (a, b) in enumerate(((k_in, k), (s_in, s), (p_in, p), (q_in, q)))]
    for c in copies:
        c.start()
    seg = lanes() % SEG // 4
    layer = lanes() // SEG
    first = [jnp.zeros((ROWS, LANES), F32) for _ in range(TILES)]
    last = [jnp.zeros((ROWS, LANES), F32) for _ in range(TILES)]
    for i, ref in enumerate((k, s, p, q)):
        copies[i].wait()
        for t in range(TILES):
            for zz in range(PER):
                x = ref[t * PER + zz]
                here = (layer == zz) & (seg == i)
                at = zz * SEG + 4 * i
                first[t] = jnp.where(here, turn(x, at, 1), first[t])
                last[t] = jnp.where(here, turn(x, at + HALO, 1), last[t])
    for t in range(TILES):
        to_prev[t] = first[t]
        to_next[t] = last[t]


def pair(at, a, b, to_far, to_near):
    odd = lax.axis_index("gx") % 2 == 1
    low = sublanes() < HALO
    before = jnp.where(low, a, turn(b, HALO, 0))
    after = jnp.where(low, turn(a, HALO, 0), b)
    to_far[at] = jnp.where(odd, after, before)
    to_near[at] = jnp.where(odd, before, after)


def pack_body(k, s, p, q, to_far, to_near):
    for z in range(NZ):
        pair(z, k[z], s[z], to_far, to_near)
        pair(NZ + z, p[z], q[z], to_far, to_near)


def pack_strip(own_first, own_last, from_prev, from_next, packed, to_far, to_near):
    seg = lanes() % SEG // 4
    for t in range(TILES):
        cols = []
        for i in range(4):
            x = turn(from_prev[t], -4 * i, 1)
            x = jnp.where(seg == 1, turn(own_first[t], 4 - 4 * i, 1), x)
            x = jnp.where(seg == 2, turn(own_last[t], 8 - 4 * i, 1), x)
            x = jnp.where(seg == 3, turn(from_next[t], 12 - 4 * i, 1), x)
            packed[i, t] = x
            cols.append(x)
        pair(t, cols[0], cols[1], to_far, to_near)
        pair(TILES + t, cols[2], cols[3], to_far, to_near)


def layer_next(x):
    edge = lanes((SPAN, LANES)) < LANES - SEG
    moved = [turn(t, -SEG, 1) for t in x]
    return [jnp.where(edge, moved[i], moved[(i + 1) % TILES]) for i in range(TILES)]


def layer_prev(x):
    edge = lanes((SPAN, LANES)) >= SEG
    moved = [turn(t, SEG, 1) for t in x]
    return [jnp.where(edge, moved[i], moved[(i - 1) % TILES]) for i in range(TILES)]


def each(f, *args):
    return [f(*a) for a in zip(*args)]


def packed_divergence(flows):
    fx, fy, fz = flows
    return each(lambda x, xp, y, yp, z, zp: (z - zp) + (x - xp) + (y - yp), fx, each(row_prev, fx), fy, each(col_prev, fy), fz, layer_prev(fz))


def packed_flows(terms, v):
    nexts = (each(row_next, v), each(col_next, v), layer_next(v))
    return [each(lambda c, a, b: c * (a - b), term, v, n) for term, n in zip(terms, nexts)]


def edge_next(y, packed_face, z):
    at = LANES - 1 - (z % PER * SEG + 11)
    return jnp.where(lanes((SPAN, LANES)) == LANES - 1, pltpu.roll(packed_face[z // PER], at, 1), y)


def edge_prev(y, packed_face, z):
    at = LANES - (z % PER * SEG + 3)
    return jnp.where(lanes((SPAN, LANES)) == 0, pltpu.roll(packed_face[z // PER], at, 1), col_prev(y))


def rows_inside():
    gx = lax.axis_index("gx")
    below = jnp.where(gx == lax.axis_size("gx") - 1, 0.0, 1.0)
    return jnp.where(sublanes() < HALO, below, jnp.where(gx == 0, 0.0, 1.0))


def cols_inside():
    gy = lax.axis_index("gy")
    after = jnp.where(gy == lax.axis_size("gy") - 1, 0.0, 1.0)
    seg = lanes() % SEG // 4
    return jnp.where(seg == 0, jnp.where(gy == 0, 0.0, 1.0), jnp.where(seg == 3, after, 1.0))


def halo_rows(at, far, near):
    odd = lax.axis_index("gx") % 2 == 1
    low = sublanes() < HALO
    below, above = jnp.where(odd, far[at], near[at]), jnp.where(odd, near[at], far[at])
    return jnp.where(low, below, turn(above, HALO, 0)), jnp.where(low, turn(below, HALO, 0), above)


def interior(k_own, s_own, p_own, q_own, far, near, s, q, f0, cx, cy, cz, diag, r, fpx, fpy, fpz, k, p, m):
    inside_rows = rows_inside()

    def assemble(z, _):
        ka, sa = halo_rows(z, far, near)
        pa, qa = halo_rows(NZ + z, far, near)
        k[z, :ROWS], k[z, ROWS:] = k_own[z], ka * inside_rows
        p[z, :ROWS], p[z, ROWS:] = p_own[z], pa
        q[z, :ROWS], q[z, ROWS:] = q_own[z], qa
        sat = jnp.concatenate([s_own[z], sa], 0)
        mobile = total_mobility(sat)
        s[z], m[z], f0[z] = sat, mobile, sat * sat / water_viscosity / mobile
        return _

    lax.fori_loop(0, NZ, assemble, 0, unroll=NZ // 2)
    last = lanes((SPAN, LANES)) == LANES - 1

    def first(z, carry):
        cz_prev, fz_prev = carry
        up = jnp.minimum(z + 1, NZ - 1)
        kz, pz, mz = k[z], p[z], m[z]
        ax = coefficient(kz, row_next(kz), mz, row_next(mz))
        ay = jnp.where(last, 0.0, coefficient(kz, col_next(kz), mz, col_next(mz)))
        az = jnp.where(z < NZ - 1, vertical_ratio, 0.0) * coefficient(kz, k[up], mz, m[up])
        fx = ax * (pz - row_next(pz))
        fy = ay * (pz - col_next(pz))
        fzz = az * (pz - p[up])
        diag[z] = storage_term + (az + cz_prev) + (ax + row_prev(ax)) + (ay + col_prev(ay))
        r[z] = q[z] - ((fzz - fz_prev) + (fx - row_prev(fx)) + (fy - col_prev(fy)))
        cx[z], cy[z], cz[z] = ax, ay, az
        fpx[z], fpy[z], fpz[z] = fx, fy, fzz
        return az, fzz

    zero = jnp.zeros((SPAN, LANES), F32)
    lax.fori_loop(0, NZ, first, (zero, zero), unroll=NZ // 2)


def middle(cx, cy_in, cz, diag, r_in, fpy_in, packed, far_strip, near_strip,
           sums, z0, v, fpy, fz, fv, s_pack, q_pack, fp_pack, fz_pack, fv_pack,
           cy, inv, r, cy_pack):
    inside_rows, inside_cols = rows_inside(), cols_inside()
    kp, sp, pp, qp = [], [], [], []
    for t in range(TILES):
        ka, sa = halo_rows(t, far_strip, near_strip)
        pa, qa = halo_rows(TILES + t, far_strip, near_strip)
        kp.append(jnp.concatenate([packed[0, t] * inside_cols, ka * inside_rows * inside_cols], 0))
        sp.append(jnp.concatenate([packed[1, t], sa], 0))
        pp.append(jnp.concatenate([packed[2, t], pa], 0))
        qp.append(jnp.concatenate([packed[3, t], qa], 0))
    mp = each(total_mobility, sp)
    tx = each(coefficient, kp, each(row_next, kp), mp, each(row_next, mp))
    ty = each(coefficient, kp, each(col_next, kp), mp, each(col_next, mp))
    tz = each(coefficient, kp, layer_next(kp), mp, layer_next(mp))
    tz = each(lambda c: vertical_ratio * c, tz)
    tz[-1] = jnp.where(lanes((SPAN, LANES)) < LANES - SEG, tz[-1], 0.0)
    terms = (tx, ty, tz)
    dsum = each(lambda x, xp, y, yp, z, zp: storage_term + (z + zp) + (x + xp) + (y + yp), tx, each(row_prev, tx), ty, each(col_prev, ty), tz, layer_prev(tz))
    ip = each(lambda d: 1.0 / d, dsum)
    flows_p = packed_flows(terms, pp)
    rp = each(lambda a, d: a - d, qp, packed_divergence(flows_p))
    zp0 = each(lambda a, b: a * b, rp, ip)
    flows_z = packed_flows(terms, zp0)
    gp = each(lambda a, d: storage_term * a + d, zp0, packed_divergence(flows_z))
    vp = each(lambda a, b, c: (a - b) * c, gp, rp, ip)
    flows_v = packed_flows(terms, vp)
    for t in range(TILES):
        s_pack[t], q_pack[t], cy_pack[t] = sp[t], qp[t], ty[t]
        for d in range(3):
            fp_pack[d, t], fz_pack[d, t], fv_pack[d, t] = flows_p[d][t], flows_z[d][t], flows_v[d][t]

    lane = lanes((SPAN, LANES))

    def ends(packed_face, z):
        at = z % PER * SEG
        face = packed_face[z // PER]
        return pltpu.roll(face, LANES - 1 - (at + 11), 1), pltpu.roll(face, LANES - (at + 3), 1)

    def first(z, _):
        after, before = ends(cy_pack, z)
        out, into = ends(fp_pack.at[1], z)
        last = lane == LANES - 1
        cy[z] = jnp.where(last, after, cy_in[z])
        fpy[z] = jnp.where(last, out, fpy_in[z])
        inverse = 1.0 / (diag[z] + jnp.where(last, after, jnp.where(lane == 0, before, 0.0)))
        res = r_in[z] - jnp.where(last, out, jnp.where(lane == 0, -into, 0.0))
        inv[z], r[z], z0[z] = inverse, res, res * inverse
        return _

    zero = jnp.zeros((SPAN, LANES), F32)
    zero8 = jnp.zeros((ROWS, LANES), F32)
    lax.fori_loop(0, NZ, first, 0, unroll=NZ)

    def second(z, carry):
        fz_prev, rz, zaz, rv, vaz = carry
        up = jnp.minimum(z + 1, NZ - 1)
        a = z0[z]
        fx = cx[z] * (a - row_next(a))
        fy = edge_next(cy[z] * (a - col_next(a)), fz_pack.at[1], z)
        fzz = cz[z] * (a - z0[up])
        g = storage_term * a + ((fzz - fz_prev) + (fx - row_prev(fx)) + (fy - edge_prev(fy, fz_pack.at[1], z)))
        fz[0, z], fz[1, z], fz[2, z] = fx, fy, fzz
        diff = g - r[z]
        b = diff * inv[z]
        v[z] = b
        a8, g8, d8, b8, r8 = a[:ROWS], g[:ROWS], diff[:ROWS], b[:ROWS], r[z, :ROWS]
        return fzz, rz + r8 * a8, zaz + a8 * g8, rv + a8 * d8, vaz + b8 * g8

    _, rz, zaz, rv, vaz = lax.fori_loop(0, NZ, second, (zero, zero8, zero8, zero8, zero8), unroll=NZ)

    def third(z, carry):
        fz_prev, vav = carry
        up = jnp.minimum(z + 1, NZ - 1)
        a = v[z]
        fx = cx[z] * (a - row_next(a))
        fy = edge_next(cy[z] * (a - col_next(a)), fv_pack.at[1], z)
        fzz = cz[z] * (a - v[up])
        fv[0, z], fv[1, z], fv[2, z] = fx, fy, fzz
        w = storage_term * a + ((fzz - fz_prev) + (fx - row_prev(fx)) + (fy - edge_prev(fy, fv_pack.at[1], z)))
        return fzz, vav + a[:ROWS] * w[:ROWS]

    _, vav = lax.fori_loop(0, NZ, third, (zero, zero8), unroll=NZ)
    row = zero8
    for i, x in enumerate((rz, zaz, rv, vaz, vav)):
        row = jnp.where(lanes() == i, jnp.sum(x), row)
    for i in range(sums.shape[0] // ROWS):
        sums[i * ROWS:(i + 1) * ROWS] = row


def finish(sums, p_own, z0, v, s, q, f0, fpx, fpy, fpz, fz, fv, s_pack, q_pack, fp_pack, fz_pack, fv_pack,
           pressure_out, s_out, flow, f1, s1, wy0_pack, wy1_pack, pressure, s_new, sems):
    total = jnp.sum(sums[...], axis=0, keepdims=True)
    lane = lanes((1, LANES))
    rz, zaz, rv, vaz, vav = (jnp.sum(jnp.where(lane == i, total, 0.0), axis=1, keepdims=True) for i in range(5))
    ratio = vaz / zaz
    bottom = vav - ratio * vaz
    top = rv - ratio * rz
    good = bottom > 0.0
    b = jnp.where(good, top / jnp.where(good, bottom, 1.0), 0.0)
    a = rz / zaz - b * ratio
    a16, b16 = (jnp.broadcast_to(x, (SPAN, LANES)) for x in (a, b))

    def gained(rate, fraction):
        return jnp.maximum(rate, 0.0) + jnp.minimum(rate, 0.0) * fraction

    def upwind(flux, here, there):
        return flux * jnp.where(flux > 0.0, here, there)

    flows = [[fp_pack[d, t] + a16 * fz_pack[d, t] + b16 * fv_pack[d, t] for t in range(TILES)] for d in range(3)]
    s_now = [s_pack[t] for t in range(TILES)]
    q_now = [q_pack[t] for t in range(TILES)]
    for step, keep in enumerate((wy0_pack, wy1_pack)):
        fr = each(water_fraction, s_now)
        nexts = (each(row_next, fr), each(col_next, fr), layer_next(fr))
        water = [each(upwind, fl, fr, n) for fl, n in zip(flows, nexts)]
        for t in range(TILES):
            keep[t] = water[1][t]
        if step == 0:
            s_now = each(lambda x, rate, f, d: x + step_ratio * (gained(rate, f) - d), s_now, q_now, fr, packed_divergence(water))

    def first(z, wz_prev):
        up = jnp.minimum(z + 1, NZ - 1)
        fx, fy, fzz = (fp[z] + a16 * fz[d, z] + b16 * fv[d, z] for d, fp in enumerate((fpx, fpy, fpz)))
        flow[0, z], flow[1, z], flow[2, z] = fx, fy, fzz
        pressure[z] = p_own[z] + a16[:ROWS] * z0[z, :ROWS] + b16[:ROWS] * v[z, :ROWS]
        f = f0[z]
        wx = upwind(fx, f, row_next(f))
        wy = edge_next(upwind(fy, f, col_next(f)), wy0_pack, z)
        wz = upwind(fzz, f, f0[up])
        new = s[z] + step_ratio * (gained(q[z], f) - ((wz - wz_prev) + (wx - row_prev(wx)) + (wy - edge_prev(wy, wy0_pack, z))))
        s1[z] = new
        f1[z] = water_fraction(new)
        return wz

    lax.fori_loop(0, NZ, first, jnp.zeros((SPAN, LANES), F32), unroll=NZ)
    send = pltpu.make_async_copy(pressure, pressure_out, sems.at[0])
    send.start()

    def second(z, wz_prev):
        up = jnp.minimum(z + 1, NZ - 1)
        f = f1[z]
        wx = upwind(flow[0, z], f, row_next(f))
        wy = edge_next(upwind(flow[1, z], f, col_next(f)), wy1_pack, z)
        wz = upwind(flow[2, z, :ROWS], f[:ROWS], f1[up, :ROWS])
        east = (wy - edge_prev(wy, wy1_pack, z))[:ROWS]
        s_new[z] = s1[z, :ROWS] + step_ratio * (gained(q[z, :ROWS], f[:ROWS]) - ((wz - wz_prev) + (wx - row_prev(wx))[:ROWS] + east))
        return wz

    lax.fori_loop(0, NZ, second, jnp.zeros((ROWS, LANES), F32), unroll=NZ)
    send_s = pltpu.make_async_copy(s_new, s_out, sems.at[1])
    send_s.start()
    send.wait()
    send_s.wait()


VMEM = pl.BlockSpec(memory_space=pltpu.VMEM)
ANY = pl.BlockSpec(memory_space=pl.ANY)
SCRATCH = pltpu.CompilerParams(vmem_limit_bytes=8 << 20)


def call(body, outs, args, scratch=()):
    args = [pltpu.with_memory_space_constraint(x, pltpu.VMEM) for x in args]
    return pl.pallas_call(
        body,
        compiler_params=SCRATCH,
        out_shape=tuple(pltpu.VMEM(s, F32) for s in outs),
        in_specs=[VMEM] * len(args),
        out_specs=tuple(VMEM for _ in outs),
        scratch_shapes=[pltpu.VMEM(s, F32) for s in scratch],
    )(*args)


def ring(x, axis, by):
    n = lax.axis_size(axis)
    return lax.ppermute(x, axis, [(i, (i + by) % n) for i in range(n)])


def trade(x, first):
    nx, ny = lax.axis_size("gx"), lax.axis_size("gy")
    other = {}
    for i in range(first, nx - 1, 2):
        other[i], other[i + 1] = i + 1, i
    pairs = [(i * ny + j, other[i] * ny + j if i in other else i * ny + (j ^ 1)) for i in range(nx) for j in range(ny)]
    return lax.ppermute(x, ("gx", "gy"), pairs)


def one_sample(k, s, p, q):
    own = (NZ, ROWS, LANES)
    assert k.shape == own
    cols = (TILES, ROWS, LANES)
    first, last, k, s, p, q = pl.pallas_call(
        pack_columns,
        name="pack_columns",
        compiler_params=SCRATCH,
        out_shape=tuple(pltpu.VMEM(x, F32) for x in (cols, cols, own, own, own, own)),
        in_specs=[ANY] * 4,
        out_specs=(VMEM,) * 6,
        scratch_shapes=[pltpu.SemaphoreType.DMA((4,))],
    )(*(pltpu.with_memory_space_constraint(x, pltpu.HBM) for x in (k, s, p, q)))
    from_prev = ring(last, "gy", 1)
    from_next = ring(first, "gy", -1)
    body, strips = (2 * NZ, ROWS, LANES), (2 * TILES, ROWS, LANES)
    to_far, to_near = call(pack_body, (body, body), (k, s, p, q))
    far = trade(to_far, 1)
    near = trade(to_near, 0)
    packed, to_far, to_near = call(pack_strip, ((4,) + cols, strips, strips), (first, last, from_prev, from_next))
    far_strip = trade(to_far, 1)
    near_strip = trade(to_near, 0)
    field, strip = (NZ, SPAN, LANES), (TILES, SPAN, LANES)
    s, q, f0, cx, cy, cz, diag, r, fpx, fpy, fpz = call(interior, (field,) * 11, (k, s, p, q, far, near), (field,) * 3)
    size = lax.axis_size("gx") * lax.axis_size("gy")
    sums, z0, v, fpy, *rest = call(
        middle,
        ((size, LANES),) + (field,) * 3 + ((3,) + field,) * 2 + (strip,) * 2 + ((3,) + strip,) * 3,
        (cx, cy, cz, diag, r, fpy, packed, far_strip, near_strip),
        (field,) * 3 + (strip,),
    )
    sums = lax.all_to_all(sums, ("gx", "gy"), 0, 0, tiled=True)
    args = [pltpu.with_memory_space_constraint(x, pltpu.VMEM) for x in (sums, p, z0, v, s, q, f0, fpx, fpy, fpz, *rest)]
    return pl.pallas_call(
        finish,
        name="finish",
        compiler_params=SCRATCH,
        out_shape=(jax.ShapeDtypeStruct(own, F32),) * 2,
        in_specs=[VMEM] * len(args),
        out_specs=(ANY, ANY),
        scratch_shapes=[pltpu.VMEM(x, F32) for x in ((3,) + field, field, field, strip, strip, own, own)] + [pltpu.SemaphoreType.DMA((2,))],
    )(*args)


def local(permeability, saturation, pressure_old, source):
    outs = [one_sample(permeability[i], saturation[i], pressure_old[i], source) for i in range(permeability.shape[0])]
    return jnp.stack([o[0] for o in outs]), jnp.stack([o[1] for o in outs])


def solution(mesh):
    field = P(None, None, "gx", "gy")
    return jax.shard_map(local, mesh=mesh, in_specs=(field, field, field, P(None, "gx", "gy")), out_specs=(field, field), check_vma=False)
```

profile of v0, /device:TPU:1, one launch (start us, length us, event | category | flops | bytes accessed | tf_op | source)
XLA Modules:
  0.0 44.7 jit_solution(5996097433106219102)
XLA Ops:
  0.6 1.3 %pack_columns.1 = (f32[2,8,128]{2,1,0:T(8,128)S(1)}, f32[2,8,128]{2,1,0:T(8,128)S(1)}, f32[16,8,128]{2,1,0:T(8,128)S(1)}, f32[16,8,128]{2,1,0:T(8,128)S(1)}, f32...) custom-call(f32[16,8,128]{2,1,0:T(8,128)} %bitcast.11, f32[16,8,128]{2,1,0:T(8,128)} %bitcast.12, ...), custom_call_target="tpu_custom_call" | custom-call | tf_op jit(solution)/shard_map/pack_columns/pallas_call | solution.py:405
  2.0 3.3 %collective-permute-start = (f32[32,8,128]{2,1,0:T(8,128)S(1)}, f32[32,8,128]{2,1,0:T(8,128)S(1)}, u32[]{:S(2)}, u32[]{:S(2)}) collective-permute-start(f32[32,8,128]{2,1,0:T(8,128)S(1)} %get-tuple-element.41), channel_id=1, source_target_pairs={{0,1},{1,0},{2,3},{3,2},{4,5},{5,4},{6,7},{7,6},{8,9},{9,8},{10,11... | collective-permute-start | bytes 393224 | tf_op jit(solution)/shard_map/ppermute | solution.py:398
  5.2 0.2 collective-permute-start.1
  5.5 1.2 %collective-permute-start.3 = (f32[2,8,128]{2,1,0:T(8,128)S(1)}, f32[2,8,128]{2,1,0:T(8,128)S(1)}, u32[]{:S(2)}, u32[]{:S(2)}) collective-permute-start(f32[2,8,128]{2,1,0:T(8,128)S(1)} %get-tuple-element.49.own_first), channel_id=1, source_target_pairs={{0,15},{1,0},{2,1},{3,2},{4,3},{5,4},{6,5},{7,6},{8,7},{9,8},{10,9... | collective-permute-start | bytes 24584 | tf_op jit(solution)/shard_map/ppermute | solution.py:389
  6.7 1.5 %collective-permute-start.2 = (f32[2,8,128]{2,1,0:T(8,128)S(1)}, f32[2,8,128]{2,1,0:T(8,128)S(1)}, u32[]{:S(2)}, u32[]{:S(2)}) collective-permute-start(f32[2,8,128]{2,1,0:T(8,128)S(1)} %get-tuple-element.50.own_last), channel_id=1, source_target_pairs={{0,1},{1,2},{2,3},{3,4},{4,5},{5,6},{6,7},{7,8},{8,9},{9,10},{10,1... | collective-permute-start | bytes 24584 | tf_op jit(solution)/shard_map/ppermute | solution.py:389
  8.2 1.6 %collective-permute-done.3.from_next = f32[2,8,128]{2,1,0:T(8,128)S(1)} collective-permute-done((f32[2,8,128]{2,1,0:T(8,128)S(1)}, f32[2,8,128]{2,1,0:T(8,128)S(1)}, u32[]{:S(2)}, u32[]{:S(2)}) %collective-permute-start.3) | collective-permute-done | bytes 8224 | tf_op jit(solution)/shard_map/ppermute | solution.py:389
  9.8 2.2 %collective-permute-done.2.from_prev = f32[2,8,128]{2,1,0:T(8,128)S(1)} collective-permute-done((f32[2,8,128]{2,1,0:T(8,128)S(1)}, f32[2,8,128]{2,1,0:T(8,128)S(1)}, u32[]{:S(2)}, u32[]{:S(2)}) %collective-permute-start.2) | collective-permute-done | bytes 8224 | tf_op jit(solution)/shard_map/ppermute | solution.py:389
  12.1 0.1 shard_map.61
  12.2 3.7 %collective-permute-start.4 = (f32[4,8,128]{2,1,0:T(8,128)S(1)}, f32[4,8,128]{2,1,0:T(8,128)S(1)}, u32[]{:S(2)}, u32[]{:S(2)}) collective-permute-start(f32[4,8,128]{2,1,0:T(8,128)S(1)} %get-tuple-element.52), channel_id=1, source_target_pairs={{0,1},{1,0},{2,3},{3,2},{4,5},{5,4},{6,7},{7,6},{8,9},{9,8},{10,11... | collective-permute-start | bytes 49160 | tf_op jit(solution)/shard_map/ppermute | solution.py:398
  15.9 0.0 collective-permute-start.5
  15.9 0.0 collective-permute-done.far
  15.9 0.0 collective-permute-done.1.near
  15.9 0.5 %shard_map.60 = (f32[16,16,128]{2,1,0:T(8,128)S(1)}, f32[16,16,128]{2,1,0:T(8,128)S(1)}, f32[16,16,128]{2,1,0:T(8,128)S(1)}, f32[16,16,128]{2,1,0:T(8,128)S(1)},...) custom-call(f32[16,8,128]{2,1,0:T(8,128)S(1)} %get-tuple-element.37., ...), custom_call_target="tpu_custom_call" | custom-call | tf_op jit(solution)/shard_map/pallas_call | solution.py:377
  16.4 0.3 collective-permute-done.4.far_strip
  16.7 1.8 %collective-permute-done.5.near_strip = f32[4,8,128]{2,1,0:T(8,128)S(1)} collective-permute-done((f32[4,8,128]{2,1,0:T(8,128)S(1)}, f32[4,8,128]{2,1,0:T(8,128)S(1)}, u32[]{:S(2)}, u32[]{:S(2)}) %collective-permute-start.5) | collective-permute-done | bytes 16416 | tf_op jit(solution)/shard_map/ppermute | solution.py:398
  18.5 0.9 %shard_map.62 = (f32[256,128]{1,0:T(8,128)S(1)}, f32[16,16,128]{2,1,0:T(8,128)S(1)}, f32[16,16,128]{2,1,0:T(8,128)S(1)}, f32[16,16,128]{2,1,0:T(8,128)S(1)}, f32...) custom-call(f32[16,16,128]{2,1,0:T(8,128)S(1)} %get-tuple-element.43, ...), custom_call_target="tpu_custom_call" | custom-call | tf_op jit(solution)/shard_map/pallas_call | solution.py:377
  19.4 24.1 %all_to_all.11 = f32[256,1,128]{2,1,0:T(1,128)S(1)} all-to-all(f32[256,1,128]{2,1,0:T(1,128)S(1)} %bitcast.10), channel_id=1, replica_groups=mesh['gx'=16,'gy'=16] {'gx','gy'}, dimensions={0} | all-to-all | bytes 262144 | tf_op jit(solution)/shard_map/all_to_all | solution.py:432
  43.5 1.2 %finish.1 = (f32[16,8,128]{2,1,0:T(8,128)}, f32[16,8,128]{2,1,0:T(8,128)}) custom-call(f32[256,128]{1,0:T(8,128)S(1)} %bitcast.9, f32[16,8,128]{2,1,0:T(8,128)S(1)} %get-tuple-element.39.p.p_own, f32[16,16,128]{2,1,0:T(8,128)S(1)} %get-tuple-element.55.z0, f32[16,16,128]{2,1,0:T(8,128)S(1)} %get-tuple-element.56.v, f32[16,16,128]{2,1,0:T(8,128)S(1)} %get-tuple-element.57.s, ...), custom_call_target="tpu_custom_call" | custom-call | tf_op jit(solution)/shard_map/finish/pallas_call | solution.py:434
  (1 shorter events, 0.0 us)
Async XLA Ops:
  2.0 13.9 %collective-permute-start = (f32[32,8,128]{2,1,0:T(8,128)S(1)}, f32[32,8,128]{2,1,0:T(8,128)S(1)}, u32[]{:S(2)}, u32[]{:S(2)}) collective-permute-start(f32[32,8,128]{2,1,0:T(8,128)S(1)} %get-tuple-element.41), channel_id=1, source_target_pairs={{0,1},{1,0},{2,3},{3,2},{4,5},{5,4},{6,7},{7,6},{8,9},{9,8},{10,11... | collective-permute-start | bytes 393224 | tf_op jit(solution)/shard_map/ppermute | solution.py:398
  5.2 10.7 %collective-permute-start.1 = (f32[32,8,128]{2,1,0:T(8,128)S(1)}, f32[32,8,128]{2,1,0:T(8,128)S(1)}, u32[]{:S(2)}, u32[]{:S(2)}) collective-permute-start(f32[32,8,128]{2,1,0:T(8,128)S(1)} %get-tuple-element.42), channel_id=1, source_target_pairs={{0,16},{1,17},{2,18},{3,19},{4,20},{5,21},{6,22},{7,23},{8,24},{9,... | collective-permute-start | bytes 393224 | tf_op jit(solution)/shard_map/ppermute | solution.py:398
  5.5 4.4 %collective-permute-start.3 = (f32[2,8,128]{2,1,0:T(8,128)S(1)}, f32[2,8,128]{2,1,0:T(8,128)S(1)}, u32[]{:S(2)}, u32[]{:S(2)}) collective-permute-start(f32[2,8,128]{2,1,0:T(8,128)S(1)} %get-tuple-element.49.own_first), channel_id=1, source_target_pairs={{0,15},{1,0},{2,1},{3,2},{4,3},{5,4},{6,5},{7,6},{8,7},{9,8},{10,9... | collective-permute-start | bytes 24584 | tf_op jit(solution)/shard_map/ppermute | solution.py:389
  6.7 5.4 %collective-permute-start.2 = (f32[2,8,128]{2,1,0:T(8,128)S(1)}, f32[2,8,128]{2,1,0:T(8,128)S(1)}, u32[]{:S(2)}, u32[]{:S(2)}) collective-permute-start(f32[2,8,128]{2,1,0:T(8,128)S(1)} %get-tuple-element.50.own_last), channel_id=1, source_target_pairs={{0,1},{1,2},{2,3},{3,4},{4,5},{5,6},{6,7},{7,8},{8,9},{9,10},{10,1... | collective-permute-start | bytes 24584 | tf_op jit(solution)/shard_map/ppermute | solution.py:389
  12.2 4.5 %collective-permute-start.4 = (f32[4,8,128]{2,1,0:T(8,128)S(1)}, f32[4,8,128]{2,1,0:T(8,128)S(1)}, u32[]{:S(2)}, u32[]{:S(2)}) collective-permute-start(f32[4,8,128]{2,1,0:T(8,128)S(1)} %get-tuple-element.52), channel_id=1, source_target_pairs={{0,1},{1,0},{2,3},{3,2},{4,5},{5,4},{6,7},{7,6},{8,9},{9,8},{10,11... | collective-permute-start | bytes 49160 | tf_op jit(solution)/shard_map/ppermute | solution.py:398
  15.9 2.6 %collective-permute-start.5 = (f32[4,8,128]{2,1,0:T(8,128)S(1)}, f32[4,8,128]{2,1,0:T(8,128)S(1)}, u32[]{:S(2)}, u32[]{:S(2)}) collective-permute-start(f32[4,8,128]{2,1,0:T(8,128)S(1)} %get-tuple-element.53), channel_id=1, source_target_pairs={{0,16},{1,17},{2,18},{3,19},{4,20},{5,21},{6,22},{7,23},{8,24},{9,... | collective-permute-start | bytes 49160 | tf_op jit(solution)/shard_map/ppermute | solution.py:398
where the time goes:
time: 44.9 us; the launch traced here: 44.7 us
  blocking collectives  24.1 us (54%)
  starting transfers between devices  9.97 us (22%)
  waiting for transfers between devices  5.95 us (13%)
  Pallas kernels  3.99 us (9%)
  between operations  0.68 us (2%)
    all_to_all x1, blocking collectives, one_sample(): sums = lax.all_to_all(sums, ('gx', 'gy'), 0, 0, tiled=True)  24.1 us
    ppermute x4, starting transfers between devices, trade(): return lax.ppermute(x, ('gx', 'gy'), pairs)  7.21 us
    ppermute x2, waiting for transfers between devices, ring(): return lax.ppermute(x, axis, [(i, (i + by) % n) for i in range(n)])  3.87 us
    ppermute x2, starting transfers between devices, ring(): return lax.ppermute(x, axis, [(i, (i + by) % n) for i in range(n)])  2.76 us
    ppermute x4, waiting for transfers between devices, trade(): return lax.ppermute(x, ('gx', 'gy'), pairs)  2.07 us
    pallas_call x4, Pallas kernels, call(): pl.pallas_call(body, compiler_params=SCRATCH, out_shape=tuple((pltpu.VMEM...  1.51 us
    pallas_call x1, Pallas kernels, one_sample(): pl.pallas_call(pack_columns, name='pack_columns', compiler_params=SCRATCH...  1.28 us
    pallas_call x1, Pallas kernels, one_sample(): pl.pallas_call(finish, name='finish', compiler_params=SCRATCH, out_shape=...  1.2 us
  transfers between devices with their start and end apart: 6, of which 4 were waited for; matrix products, arithmetic and copies ran while one was open for 0% of the time, Pallas kernels for 1%

commit v1 on v0

--- a/solution.py
+++ b/solution.py
@@ -69,8 +69,8 @@
     copies = [pltpu.make_async_copy(a, b, sems.at[i]) for i, (a, b) in enumerate(((k_in, k), (s_in, s), (p_in, p), (q_in, q)))]
     for c in copies:
         c.start()
-    seg = lanes() % SEG // 4
-    layer = lanes() // SEG
+    quad = lanes() // 4
+    quads = LANES // 4
     first = [jnp.zeros((ROWS, LANES), F32) for _ in range(TILES)]
     last = [jnp.zeros((ROWS, LANES), F32) for _ in range(TILES)]
     for i, ref in enumerate((k, s, p, q)):
@@ -78,12 +78,12 @@
         for t in range(TILES):
             for zz in range(PER):
                 x = ref[t * PER + zz]
-                here = (layer == zz) & (seg == i)
-                at = zz * SEG + 4 * i
-                first[t] = jnp.where(here, turn(x, at, 1), first[t])
-                last[t] = jnp.where(here, turn(x, at + HALO, 1), last[t])
+                at = zz * 4 + i
+                x = turn(x, 4 * at + HALO, 1)
+                last[t] = jnp.where(quad == at, x, last[t])
+                first[t] = jnp.where(quad == (at + 1) % quads, x, first[t])
     for t in range(TILES):
-        to_prev[t] = first[t]
+        to_prev[t] = turn(first[t], -HALO, 1)
         to_next[t] = last[t]
 
 
@@ -143,14 +143,21 @@
     return [each(lambda c, a, b: c * (a - b), term, v, n) for term, n in zip(terms, nexts)]
 
 
-def edge_next(y, packed_face, z):
-    at = LANES - 1 - (z % PER * SEG + 11)
-    return jnp.where(lanes((SPAN, LANES)) == LANES - 1, pltpu.roll(packed_face[z // PER], at, 1), y)
-
-
-def edge_prev(y, packed_face, z):
-    at = LANES - (z % PER * SEG + 3)
-    return jnp.where(lanes((SPAN, LANES)) == 0, pltpu.roll(packed_face[z // PER], at, 1), col_prev(y))
+def join_ends(face):
+    behind = lanes((SPAN, LANES)) % SEG == 11
+    return jnp.where(behind, face, turn(face, 9, 1))
+
+
+def ends(joined, z):
+    return pltpu.roll(joined[z // PER], LANES - 1 - (z % PER * SEG + 11), 1)
+
+
+def edge_next(y, end):
+    return jnp.where(lanes((SPAN, LANES)) == LANES - 1, end, y)
+
+
+def edge_prev(y, end):
+    return jnp.where(lanes((SPAN, LANES)) == 0, end, col_prev(y))
 
 
 def rows_inside():
@@ -212,7 +219,7 @@
 
 def middle(cx, cy_in, cz, diag, r_in, fpy_in, packed, far_strip, near_strip,
            sums, z0, v, fpy, fz, fv, s_pack, q_pack, fp_pack, fz_pack, fv_pack,
-           cy, inv, r, cy_pack):
+           cy, inv, r, cy_ends, fp_ends, fz_ends, fv_ends):
     inside_rows, inside_cols = rows_inside(), cols_inside()
     kp, sp, pp, qp = [], [], [], []
     for t in range(TILES):
@@ -239,25 +246,21 @@
     vp = each(lambda a, b, c: (a - b) * c, gp, rp, ip)
     flows_v = packed_flows(terms, vp)
     for t in range(TILES):
-        s_pack[t], q_pack[t], cy_pack[t] = sp[t], qp[t], ty[t]
+        s_pack[t], q_pack[t] = sp[t], qp[t]
+        for joined, face in ((cy_ends, ty), (fp_ends, flows_p[1]), (fz_ends, flows_z[1]), (fv_ends, flows_v[1])):
+            joined[t] = join_ends(face[t])
         for d in range(3):
             fp_pack[d, t], fz_pack[d, t], fv_pack[d, t] = flows_p[d][t], flows_z[d][t], flows_v[d][t]
 
     lane = lanes((SPAN, LANES))
 
-    def ends(packed_face, z):
-        at = z % PER * SEG
-        face = packed_face[z // PER]
-        return pltpu.roll(face, LANES - 1 - (at + 11), 1), pltpu.roll(face, LANES - (at + 3), 1)
-
     def first(z, _):
-        after, before = ends(cy_pack, z)
-        out, into = ends(fp_pack.at[1], z)
+        c, f = ends(cy_ends, z), ends(fp_ends, z)
         last = lane == LANES - 1
-        cy[z] = jnp.where(last, after, cy_in[z])
-        fpy[z] = jnp.where(last, out, fpy_in[z])
-        inverse = 1.0 / (diag[z] + jnp.where(last, after, jnp.where(lane == 0, before, 0.0)))
-        res = r_in[z] - jnp.where(last, out, jnp.where(lane == 0, -into, 0.0))
+        cy[z] = jnp.where(last, c, cy_in[z])
+        fpy[z] = jnp.where(last, f, fpy_in[z])
+        inverse = 1.0 / (diag[z] + jnp.where(last | (lane == 0), c, 0.0))
+        res = r_in[z] - jnp.where(last, f, jnp.where(lane == 0, -f, 0.0))
         inv[z], r[z], z0[z] = inverse, res, res * inverse
         return _
 
@@ -270,9 +273,10 @@
         up = jnp.minimum(z + 1, NZ - 1)
         a = z0[z]
         fx = cx[z] * (a - row_next(a))
-        fy = edge_next(cy[z] * (a - col_next(a)), fz_pack.at[1], z)
+        end = ends(fz_ends, z)
+        fy = edge_next(cy[z] * (a - col_next(a)), end)
         fzz = cz[z] * (a - z0[up])
-        g = storage_term * a + ((fzz - fz_prev) + (fx - row_prev(fx)) + (fy - edge_prev(fy, fz_pack.at[1], z)))
+        g = storage_term * a + ((fzz - fz_prev) + (fx - row_prev(fx)) + (fy - edge_prev(fy, end)))
         fz[0, z], fz[1, z], fz[2, z] = fx, fy, fzz
         diff = g - r[z]
         b = diff * inv[z]
@@ -287,10 +291,11 @@
         up = jnp.minimum(z + 1, NZ - 1)
         a = v[z]
         fx = cx[z] * (a - row_next(a))
-        fy = edge_next(cy[z] * (a - col_next(a)), fv_pack.at[1], z)
+        end = ends(fv_ends, z)
+        fy = edge_next(cy[z] * (a - col_next(a)), end)
         fzz = cz[z] * (a - v[up])
         fv[0, z], fv[1, z], fv[2, z] = fx, fy, fzz
-        w = storage_term * a + ((fzz - fz_prev) + (fx - row_prev(fx)) + (fy - edge_prev(fy, fv_pack.at[1], z)))
+        w = storage_term * a + ((fzz - fz_prev) + (fx - row_prev(fx)) + (fy - edge_prev(fy, end)))
         return fzz, vav + a[:ROWS] * w[:ROWS]
 
     _, vav = lax.fori_loop(0, NZ, third, (zero, zero8), unroll=NZ)
@@ -302,7 +307,7 @@
 
 
 def finish(sums, p_own, z0, v, s, q, f0, fpx, fpy, fpz, fz, fv, s_pack, q_pack, fp_pack, fz_pack, fv_pack,
-           pressure_out, s_out, flow, f1, s1, wy0_pack, wy1_pack, pressure, s_new, sems):
+           pressure_out, s_out, flow, f1, s1, wy0_ends, wy1_ends, pressure, s_new, sems):
     total = jnp.sum(sums[...], axis=0, keepdims=True)
     lane = lanes((1, LANES))
     rz, zaz, rv, vaz, vav = (jnp.sum(jnp.where(lane == i, total, 0.0), axis=1, keepdims=True) for i in range(5))
@@ -323,12 +328,12 @@
     flows = [[fp_pack[d, t] + a16 * fz_pack[d, t] + b16 * fv_pack[d, t] for t in range(TILES)] for d in range(3)]
     s_now = [s_pack[t] for t in range(TILES)]
     q_now = [q_pack[t] for t in range(TILES)]
-    for step, keep in enumerate((wy0_pack, wy1_pack)):
+    for step, keep in enumerate((wy0_ends, wy1_ends)):
         fr = each(water_fraction, s_now)
         nexts = (each(row_next, fr), each(col_next, fr), layer_next(fr))
         water = [each(upwind, fl, fr, n) for fl, n in zip(flows, nexts)]
         for t in range(TILES):
-            keep[t] = water[1][t]
+            keep[t] = join_ends(water[1][t])
         if step == 0:
             s_now = each(lambda x, rate, f, d: x + step_ratio * (gained(rate, f) - d), s_now, q_now, fr, packed_divergence(water))
 
@@ -339,9 +344,10 @@
         pressure[z] = p_own[z] + a16[:ROWS] * z0[z, :ROWS] + b16[:ROWS] * v[z, :ROWS]
         f = f0[z]
         wx = upwind(fx, f, row_next(f))
-        wy = edge_next(upwind(fy, f, col_next(f)), wy0_pack, z)
+        end = ends(wy0_ends, z)
+        wy = edge_next(upwind(fy, f, col_next(f)), end)
         wz = upwind(fzz, f, f0[up])
-        new = s[z] + step_ratio * (gained(q[z], f) - ((wz - wz_prev) + (wx - row_prev(wx)) + (wy - edge_prev(wy, wy0_pack, z))))
+        new = s[z] + step_ratio * (gained(q[z], f) - ((wz - wz_prev) + (wx - row_prev(wx)) + (wy - edge_prev(wy, end))))
         s1[z] = new
         f1[z] = water_fraction(new)
         return wz
@@ -354,9 +360,10 @@
         up = jnp.minimum(z + 1, NZ - 1)
         f = f1[z]
         wx = upwind(flow[0, z], f, row_next(f))
-        wy = edge_next(upwind(flow[1, z], f, col_next(f)), wy1_pack, z)
+        end = ends(wy1_ends, z)
+        wy = edge_next(upwind(flow[1, z], f, col_next(f)), end)
         wz = upwind(flow[2, z, :ROWS], f[:ROWS], f1[up, :ROWS])
-        east = (wy - edge_prev(wy, wy1_pack, z))[:ROWS]
+        east = (wy - edge_prev(wy, end))[:ROWS]
         s_new[z] = s1[z, :ROWS] + step_ratio * (gained(q[z, :ROWS], f[:ROWS]) - ((wz - wz_prev) + (wx - row_prev(wx))[:ROWS] + east))
         return wz
 
@@ -427,7 +434,7 @@
         middle,
         ((size, LANES),) + (field,) * 3 + ((3,) + field,) * 2 + (strip,) * 2 + ((3,) + strip,) * 3,
         (cx, cy, cz, diag, r, fpy, packed, far_strip, near_strip),
-        (field,) * 3 + (strip,),
+        (field,) * 3 + (strip,) * 4,
     )
     sums = lax.all_to_all(sums, ("gx", "gy"), 0, 0, tiled=True)
     args = [pltpu.with_memory_space_constraint(x, pltpu.VMEM) for x in (sums, p, z0, v, s, q, f0, fpx, fpy, fpz, *rest)]

time: 44.9 us -> 44.9 us (level)
  no operation moved by 1% of the time
where the time goes in v1:
time: 44.9 us; the launch traced here: 44.7 us
  blocking collectives  24.1 us (54%)
  starting transfers between devices  9.97 us (22%)
  waiting for transfers between devices  5.95 us (13%)
  Pallas kernels  4.01 us (9%)
  between operations  0.68 us (2%)
    all_to_all x1, blocking collectives, one_sample(): sums = lax.all_to_all(sums, ('gx', 'gy'), 0, 0, tiled=True)  24.1 us
    ppermute x4, starting transfers between devices, trade(): return lax.ppermute(x, ('gx', 'gy'), pairs)  7.21 us
    ppermute x2, waiting for transfers between devices, ring(): return lax.ppermute(x, axis, [(i, (i + by) % n) for i in range(n)])  3.87 us
    ppermute x2, starting transfers between devices, ring(): return lax.ppermute(x, axis, [(i, (i + by) % n) for i in range(n)])  2.76 us
    ppermute x4, waiting for transfers between devices, trade(): return lax.ppermute(x, ('gx', 'gy'), pairs)  2.07 us
    pallas_call x4, Pallas kernels, call(): pl.pallas_call(body, compiler_params=SCRATCH, out_shape=tuple((pltpu.VMEM...  1.52 us
    pallas_call x1, Pallas kernels, one_sample(): pl.pallas_call(pack_columns, name='pack_columns', compiler_params=SCRATCH...  1.28 us
    pallas_call x1, Pallas kernels, one_sample(): pl.pallas_call(finish, name='finish', compiler_params=SCRATCH, out_shape=...  1.21 us
  transfers between devices with their start and end apart: 6, of which 4 were waited for; matrix products, arithmetic and copies ran while one was open for 0% of the time, Pallas kernels for 1%

profile of v1, /device:TPU:1, one launch (start us, length us, event | category | flops | bytes accessed | tf_op | source)
XLA Modules:
  0.0 44.7 jit_solution(14580317902140209559)
XLA Ops:
  0.6 1.3 %pack_columns.1 = (f32[2,8,128]{2,1,0:T(8,128)S(1)}, f32[2,8,128]{2,1,0:T(8,128)S(1)}, f32[16,8,128]{2,1,0:T(8,128)S(1)}, f32[16,8,128]{2,1,0:T(8,128)S(1)}, f32...) custom-call(f32[16,8,128]{2,1,0:T(8,128)} %bitcast.11, f32[16,8,128]{2,1,0:T(8,128)} %bitcast.12, ...), custom_call_target="tpu_custom_call" | custom-call | tf_op jit(solution)/shard_map/pack_columns/pallas_call | solution.py:412
  2.0 3.3 %collective-permute-start = (f32[32,8,128]{2,1,0:T(8,128)S(1)}, f32[32,8,128]{2,1,0:T(8,128)S(1)}, u32[]{:S(2)}, u32[]{:S(2)}) collective-permute-start(f32[32,8,128]{2,1,0:T(8,128)S(1)} %get-tuple-element.41), channel_id=1, source_target_pairs={{0,1},{1,0},{2,3},{3,2},{4,5},{5,4},{6,7},{7,6},{8,9},{9,8},{10,11... | collective-permute-start | bytes 393224 | tf_op jit(solution)/shard_map/ppermute | solution.py:405
  5.3 0.2 collective-permute-start.1
  5.5 1.2 %collective-permute-start.3 = (f32[2,8,128]{2,1,0:T(8,128)S(1)}, f32[2,8,128]{2,1,0:T(8,128)S(1)}, u32[]{:S(2)}, u32[]{:S(2)}) collective-permute-start(f32[2,8,128]{2,1,0:T(8,128)S(1)} %get-tuple-element.49.own_first), channel_id=1, source_target_pairs={{0,15},{1,0},{2,1},{3,2},{4,3},{5,4},{6,5},{7,6},{8,7},{9,8},{10,9... | collective-permute-start | bytes 24584 | tf_op jit(solution)/shard_map/ppermute | solution.py:396
  6.7 1.5 %collective-permute-start.2 = (f32[2,8,128]{2,1,0:T(8,128)S(1)}, f32[2,8,128]{2,1,0:T(8,128)S(1)}, u32[]{:S(2)}, u32[]{:S(2)}) collective-permute-start(f32[2,8,128]{2,1,0:T(8,128)S(1)} %get-tuple-element.50.own_last), channel_id=1, source_target_pairs={{0,1},{1,2},{2,3},{3,4},{4,5},{5,6},{6,7},{7,8},{8,9},{9,10},{10,1... | collective-permute-start | bytes 24584 | tf_op jit(solution)/shard_map/ppermute | solution.py:396
  8.2 1.6 %collective-permute-done.3.from_next = f32[2,8,128]{2,1,0:T(8,128)S(1)} collective-permute-done((f32[2,8,128]{2,1,0:T(8,128)S(1)}, f32[2,8,128]{2,1,0:T(8,128)S(1)}, u32[]{:S(2)}, u32[]{:S(2)}) %collective-permute-start.3) | collective-permute-done | bytes 8224 | tf_op jit(solution)/shard_map/ppermute | solution.py:396
  9.8 2.2 %collective-permute-done.2.from_prev = f32[2,8,128]{2,1,0:T(8,128)S(1)} collective-permute-done((f32[2,8,128]{2,1,0:T(8,128)S(1)}, f32[2,8,128]{2,1,0:T(8,128)S(1)}, u32[]{:S(2)}, u32[]{:S(2)}) %collective-permute-start.2) | collective-permute-done | bytes 8224 | tf_op jit(solution)/shard_map/ppermute | solution.py:396
  12.1 0.1 shard_map.61
  12.2 3.7 %collective-permute-start.4 = (f32[4,8,128]{2,1,0:T(8,128)S(1)}, f32[4,8,128]{2,1,0:T(8,128)S(1)}, u32[]{:S(2)}, u32[]{:S(2)}) collective-permute-start(f32[4,8,128]{2,1,0:T(8,128)S(1)} %get-tuple-element.52), channel_id=1, source_target_pairs={{0,1},{1,0},{2,3},{3,2},{4,5},{5,4},{6,7},{7,6},{8,9},{9,8},{10,11... | collective-permute-start | bytes 49160 | tf_op jit(solution)/shard_map/ppermute | solution.py:405
  15.9 0.0 collective-permute-start.5
  15.9 0.0 collective-permute-done.far
  15.9 0.0 collective-permute-done.1.near
  15.9 0.5 %shard_map.60 = (f32[16,16,128]{2,1,0:T(8,128)S(1)}, f32[16,16,128]{2,1,0:T(8,128)S(1)}, f32[16,16,128]{2,1,0:T(8,128)S(1)}, f32[16,16,128]{2,1,0:T(8,128)S(1)},...) custom-call(f32[16,8,128]{2,1,0:T(8,128)S(1)} %get-tuple-element.37., ...), custom_call_target="tpu_custom_call" | custom-call | tf_op jit(solution)/shard_map/pallas_call | solution.py:384
  16.4 0.3 collective-permute-done.4.far_strip
  16.7 1.8 %collective-permute-done.5.near_strip = f32[4,8,128]{2,1,0:T(8,128)S(1)} collective-permute-done((f32[4,8,128]{2,1,0:T(8,128)S(1)}, f32[4,8,128]{2,1,0:T(8,128)S(1)}, u32[]{:S(2)}, u32[]{:S(2)}) %collective-permute-start.5) | collective-permute-done | bytes 16416 | tf_op jit(solution)/shard_map/ppermute | solution.py:405
  18.5 0.9 %shard_map.62 = (f32[256,128]{1,0:T(8,128)S(1)}, f32[16,16,128]{2,1,0:T(8,128)S(1)}, f32[16,16,128]{2,1,0:T(8,128)S(1)}, f32[16,16,128]{2,1,0:T(8,128)S(1)}, f32...) custom-call(f32[16,16,128]{2,1,0:T(8,128)S(1)} %get-tuple-element.43, ...), custom_call_target="tpu_custom_call" | custom-call | tf_op jit(solution)/shard_map/pallas_call | solution.py:384
  19.4 24.1 %all_to_all.11 = f32[256,1,128]{2,1,0:T(1,128)S(1)} all-to-all(f32[256,1,128]{2,1,0:T(1,128)S(1)} %bitcast.10), channel_id=1, replica_groups=mesh['gx'=16,'gy'=16] {'gx','gy'}, dimensions={0} | all-to-all | bytes 262144 | tf_op jit(solution)/shard_map/all_to_all | solution.py:439
  43.5 1.2 %finish.1 = (f32[16,8,128]{2,1,0:T(8,128)}, f32[16,8,128]{2,1,0:T(8,128)}) custom-call(f32[256,128]{1,0:T(8,128)S(1)} %bitcast.9, f32[16,8,128]{2,1,0:T(8,128)S(1)} %get-tuple-element.39.p.p_own, f32[16,16,128]{2,1,0:T(8,128)S(1)} %get-tuple-element.55.z0, f32[16,16,128]{2,1,0:T(8,128)S(1)} %get-tuple-element.56.v, f32[16,16,128]{2,1,0:T(8,128)S(1)} %get-tuple-element.57.s, ...), custom_call_target="tpu_custom_call" | custom-call | tf_op jit(solution)/shard_map/finish/pallas_call | solution.py:441
  (1 shorter events, 0.0 us)
Async XLA Ops:
  2.0 13.9 %collective-permute-start = (f32[32,8,128]{2,1,0:T(8,128)S(1)}, f32[32,8,128]{2,1,0:T(8,128)S(1)}, u32[]{:S(2)}, u32[]{:S(2)}) collective-permute-start(f32[32,8,128]{2,1,0:T(8,128)S(1)} %get-tuple-element.41), channel_id=1, source_target_pairs={{0,1},{1,0},{2,3},{3,2},{4,5},{5,4},{6,7},{7,6},{8,9},{9,8},{10,11... | collective-permute-start | bytes 393224 | tf_op jit(solution)/shard_map/ppermute | solution.py:405
  5.3 10.7 %collective-permute-start.1 = (f32[32,8,128]{2,1,0:T(8,128)S(1)}, f32[32,8,128]{2,1,0:T(8,128)S(1)}, u32[]{:S(2)}, u32[]{:S(2)}) collective-permute-start(f32[32,8,128]{2,1,0:T(8,128)S(1)} %get-tuple-element.42), channel_id=1, source_target_pairs={{0,16},{1,17},{2,18},{3,19},{4,20},{5,21},{6,22},{7,23},{8,24},{9,... | collective-permute-start | bytes 393224 | tf_op jit(solution)/shard_map/ppermute | solution.py:405
  5.5 4.4 %collective-permute-start.3 = (f32[2,8,128]{2,1,0:T(8,128)S(1)}, f32[2,8,128]{2,1,0:T(8,128)S(1)}, u32[]{:S(2)}, u32[]{:S(2)}) collective-permute-start(f32[2,8,128]{2,1,0:T(8,128)S(1)} %get-tuple-element.49.own_first), channel_id=1, source_target_pairs={{0,15},{1,0},{2,1},{3,2},{4,3},{5,4},{6,5},{7,6},{8,7},{9,8},{10,9... | collective-permute-start | bytes 24584 | tf_op jit(solution)/shard_map/ppermute | solution.py:396
  6.7 5.4 %collective-permute-start.2 = (f32[2,8,128]{2,1,0:T(8,128)S(1)}, f32[2,8,128]{2,1,0:T(8,128)S(1)}, u32[]{:S(2)}, u32[]{:S(2)}) collective-permute-start(f32[2,8,128]{2,1,0:T(8,128)S(1)} %get-tuple-element.50.own_last), channel_id=1, source_target_pairs={{0,1},{1,2},{2,3},{3,4},{4,5},{5,6},{6,7},{7,8},{8,9},{9,10},{10,1... | collective-permute-start | bytes 24584 | tf_op jit(solution)/shard_map/ppermute | solution.py:396
  12.2 4.5 %collective-permute-start.4 = (f32[4,8,128]{2,1,0:T(8,128)S(1)}, f32[4,8,128]{2,1,0:T(8,128)S(1)}, u32[]{:S(2)}, u32[]{:S(2)}) collective-permute-start(f32[4,8,128]{2,1,0:T(8,128)S(1)} %get-tuple-element.52), channel_id=1, source_target_pairs={{0,1},{1,0},{2,3},{3,2},{4,5},{5,4},{6,7},{7,6},{8,9},{9,8},{10,11... | collective-permute-start | bytes 49160 | tf_op jit(solution)/shard_map/ppermute | solution.py:405
  15.9 2.6 %collective-permute-start.5 = (f32[4,8,128]{2,1,0:T(8,128)S(1)}, f32[4,8,128]{2,1,0:T(8,128)S(1)}, u32[]{:S(2)}, u32[]{:S(2)}) collective-permute-start(f32[4,8,128]{2,1,0:T(8,128)S(1)} %get-tuple-element.53), channel_id=1, source_target_pairs={{0,16},{1,17},{2,18},{3,19},{4,20},{5,21},{6,22},{7,23},{8,24},{9,... | collective-permute-start | bytes 49160 | tf_op jit(solution)/shard_map/ppermute | solution.py:405

commit v2 on v1

--- a/solution.py
+++ b/solution.py
@@ -18,6 +18,7 @@
 TILES = NZ * SEG // LANES
 PER = LANES // SEG
 F32 = jnp.float32
+PIECE = 8
 
 
 def lanes(shape=(ROWS, LANES)):
@@ -66,22 +67,28 @@
 
 
 def pack_columns(k_in, s_in, p_in, q_in, to_prev, to_next, k, s, p, q, sems):
-    copies = [pltpu.make_async_copy(a, b, sems.at[i]) for i, (a, b) in enumerate(((k_in, k), (s_in, s), (p_in, p), (q_in, q)))]
-    for c in copies:
-        c.start()
+    pieces = range(0, NZ, PIECE)
+    copies = [
+        [pltpu.make_async_copy(a.at[z:z + PIECE], b.at[z:z + PIECE], sems.at[i, z // PIECE]) for i, (a, b) in enumerate(((k_in, k), (s_in, s), (p_in, p), (q_in, q)))]
+        for z in pieces
+    ]
+    for piece in copies:
+        for c in piece:
+            c.start()
     quad = lanes() // 4
     quads = LANES // 4
     first = [jnp.zeros((ROWS, LANES), F32) for _ in range(TILES)]
     last = [jnp.zeros((ROWS, LANES), F32) for _ in range(TILES)]
-    for i, ref in enumerate((k, s, p, q)):
-        copies[i].wait()
-        for t in range(TILES):
-            for zz in range(PER):
-                x = ref[t * PER + zz]
-                at = zz * 4 + i
-                x = turn(x, 4 * at + HALO, 1)
-                last[t] = jnp.where(quad == at, x, last[t])
-                first[t] = jnp.where(quad == (at + 1) % quads, x, first[t])
+    for z in range(NZ):
+        if z % PIECE == 0:
+            for c in copies[z // PIECE]:
+                c.wait()
+        t, zz = divmod(z, PER)
+        for i, ref in enumerate((k, s, p, q)):
+            at = zz * 4 + i
+            x = turn(ref[z], 4 * at + HALO, 1)
+            last[t] = jnp.where(quad == at, x, last[t])
+            first[t] = jnp.where(quad == (at + 1) % quads, x, first[t])
     for t in range(TILES):
         to_prev[t] = turn(first[t], -HALO, 1)
         to_next[t] = last[t]
@@ -367,11 +374,14 @@
         s_new[z] = s1[z, :ROWS] + step_ratio * (gained(q[z, :ROWS], f[:ROWS]) - ((wz - wz_prev) + (wx - row_prev(wx))[:ROWS] + east))
         return wz
 
-    lax.fori_loop(0, NZ, second, jnp.zeros((ROWS, LANES), F32), unroll=NZ)
-    send_s = pltpu.make_async_copy(s_new, s_out, sems.at[1])
-    send_s.start()
-    send.wait()
-    send_s.wait()
+    carry, half, sent = jnp.zeros((ROWS, LANES), F32), NZ // 2, [send]
+    for i in range(2):
+        carry = lax.fori_loop(i * half, (i + 1) * half, second, carry, unroll=half)
+        part = slice(i * half, (i + 1) * half)
+        sent.append(pltpu.make_async_copy(s_new.at[part], s_out.at[part], sems.at[1 + i]))
+        sent[-1].start()
+    for c in sent:
+        c.wait()
 
 
 VMEM = pl.BlockSpec(memory_space=pltpu.VMEM)
@@ -416,7 +426,7 @@
         out_shape=tuple(pltpu.VMEM(x, F32) for x in (cols, cols, own, own, own, own)),
         in_specs=[ANY] * 4,
         out_specs=(VMEM,) * 6,
-        scratch_shapes=[pltpu.SemaphoreType.DMA((4,))],
+        scratch_shapes=[pltpu.SemaphoreType.DMA((4, NZ // PIECE))],
     )(*(pltpu.with_memory_space_constraint(x, pltpu.HBM) for x in (k, s, p, q)))
     from_prev = ring(last, "gy", 1)
     from_next = ring(first, "gy", -1)
@@ -445,7 +455,7 @@
         out_shape=(jax.ShapeDtypeStruct(own, F32),) * 2,
         in_specs=[VMEM] * len(args),
         out_specs=(ANY, ANY),
-        scratch_shapes=[pltpu.VMEM(x, F32) for x in ((3,) + field, field, field, strip, strip, own, own)] + [pltpu.SemaphoreType.DMA((2,))],
+        scratch_shapes=[pltpu.VMEM(x, F32) for x in ((3,) + field, field, field, strip, strip, own, own)] + [pltpu.SemaphoreType.DMA((3,))],
     )(*args)
 
 

time: 44.9 us -> 44.8 us (level)
  no operation moved by 1% of the time
where the time goes in v2:
time: 44.8 us; the launch traced here: 44.6 us
  blocking collectives  24.1 us (54%)
  starting transfers between devices  9.97 us (22%)
  waiting for transfers between devices  5.95 us (13%)
  Pallas kernels  3.88 us (9%)
  between operations  0.68 us (2%)
    all_to_all x1, blocking collectives, one_sample(): sums = lax.all_to_all(sums, ('gx', 'gy'), 0, 0, tiled=True)  24.1 us
    ppermute x4, starting transfers between devices, trade(): return lax.ppermute(x, ('gx', 'gy'), pairs)  7.21 us
    ppermute x2, waiting for transfers between devices, ring(): return lax.ppermute(x, axis, [(i, (i + by) % n) for i in range(n)])  3.87 us
    ppermute x2, starting transfers between devices, ring(): return lax.ppermute(x, axis, [(i, (i + by) % n) for i in range(n)])  2.76 us
    ppermute x4, waiting for transfers between devices, trade(): return lax.ppermute(x, ('gx', 'gy'), pairs)  2.07 us
    pallas_call x4, Pallas kernels, call(): pl.pallas_call(body, compiler_params=SCRATCH, out_shape=tuple((pltpu.VMEM...  1.52 us
    pallas_call x1, Pallas kernels, one_sample(): pl.pallas_call(finish, name='finish', compiler_params=SCRATCH, out_shape=...  1.2 us
    pallas_call x1, Pallas kernels, one_sample(): pl.pallas_call(pack_columns, name='pack_columns', compiler_params=SCRATCH...  1.15 us
  transfers between devices with their start and end apart: 6, of which 4 were waited for; matrix products, arithmetic and copies ran while one was open for 0% of the time, Pallas kernels for 1%

profile of v2, /device:TPU:1, one launch (start us, length us, event | category | flops | bytes accessed | tf_op | source)
XLA Modules:
  0.0 44.6 jit_solution(11434973400864791760)
XLA Ops:
  0.6 1.2 %pack_columns.1 = (f32[2,8,128]{2,1,0:T(8,128)S(1)}, f32[2,8,128]{2,1,0:T(8,128)S(1)}, f32[16,8,128]{2,1,0:T(8,128)S(1)}, f32[16,8,128]{2,1,0:T(8,128)S(1)}, f32...) custom-call(f32[16,8,128]{2,1,0:T(8,128)} %bitcast.11, f32[16,8,128]{2,1,0:T(8,128)} %bitcast.12, ...), custom_call_target="tpu_custom_call" | custom-call | tf_op jit(solution)/shard_map/pack_columns/pallas_call | solution.py:422
  1.8 3.3 %collective-permute-start = (f32[32,8,128]{2,1,0:T(8,128)S(1)}, f32[32,8,128]{2,1,0:T(8,128)S(1)}, u32[]{:S(2)}, u32[]{:S(2)}) collective-permute-start(f32[32,8,128]{2,1,0:T(8,128)S(1)} %get-tuple-element.41), channel_id=1, source_target_pairs={{0,1},{1,0},{2,3},{3,2},{4,5},{5,4},{6,7},{7,6},{8,9},{9,8},{10,11... | collective-permute-start | bytes 393224 | tf_op jit(solution)/shard_map/ppermute | solution.py:415
  5.1 0.2 collective-permute-start.1
  5.3 1.2 %collective-permute-start.3 = (f32[2,8,128]{2,1,0:T(8,128)S(1)}, f32[2,8,128]{2,1,0:T(8,128)S(1)}, u32[]{:S(2)}, u32[]{:S(2)}) collective-permute-start(f32[2,8,128]{2,1,0:T(8,128)S(1)} %get-tuple-element.49.own_first), channel_id=1, source_target_pairs={{0,15},{1,0},{2,1},{3,2},{4,3},{5,4},{6,5},{7,6},{8,7},{9,8},{10,9... | collective-permute-start | bytes 24584 | tf_op jit(solution)/shard_map/ppermute | solution.py:406
  6.6 1.5 %collective-permute-start.2 = (f32[2,8,128]{2,1,0:T(8,128)S(1)}, f32[2,8,128]{2,1,0:T(8,128)S(1)}, u32[]{:S(2)}, u32[]{:S(2)}) collective-permute-start(f32[2,8,128]{2,1,0:T(8,128)S(1)} %get-tuple-element.50.own_last), channel_id=1, source_target_pairs={{0,1},{1,2},{2,3},{3,4},{4,5},{5,6},{6,7},{7,8},{8,9},{9,10},{10,1... | collective-permute-start | bytes 24584 | tf_op jit(solution)/shard_map/ppermute | solution.py:406
  8.1 1.6 %collective-permute-done.3.from_next = f32[2,8,128]{2,1,0:T(8,128)S(1)} collective-permute-done((f32[2,8,128]{2,1,0:T(8,128)S(1)}, f32[2,8,128]{2,1,0:T(8,128)S(1)}, u32[]{:S(2)}, u32[]{:S(2)}) %collective-permute-start.3) | collective-permute-done | bytes 8224 | tf_op jit(solution)/shard_map/ppermute | solution.py:406
  9.7 2.2 %collective-permute-done.2.from_prev = f32[2,8,128]{2,1,0:T(8,128)S(1)} collective-permute-done((f32[2,8,128]{2,1,0:T(8,128)S(1)}, f32[2,8,128]{2,1,0:T(8,128)S(1)}, u32[]{:S(2)}, u32[]{:S(2)}) %collective-permute-start.2) | collective-permute-done | bytes 8224 | tf_op jit(solution)/shard_map/ppermute | solution.py:406
  12.0 0.1 shard_map.61
  12.1 3.7 %collective-permute-start.4 = (f32[4,8,128]{2,1,0:T(8,128)S(1)}, f32[4,8,128]{2,1,0:T(8,128)S(1)}, u32[]{:S(2)}, u32[]{:S(2)}) collective-permute-start(f32[4,8,128]{2,1,0:T(8,128)S(1)} %get-tuple-element.52), channel_id=1, source_target_pairs={{0,1},{1,0},{2,3},{3,2},{4,5},{5,4},{6,7},{7,6},{8,9},{9,8},{10,11... | collective-permute-start | bytes 49160 | tf_op jit(solution)/shard_map/ppermute | solution.py:415
  15.8 0.0 collective-permute-start.5
  15.8 0.0 collective-permute-done.far
  15.8 0.0 collective-permute-done.1.near
  15.8 0.5 %shard_map.60 = (f32[16,16,128]{2,1,0:T(8,128)S(1)}, f32[16,16,128]{2,1,0:T(8,128)S(1)}, f32[16,16,128]{2,1,0:T(8,128)S(1)}, f32[16,16,128]{2,1,0:T(8,128)S(1)},...) custom-call(f32[16,8,128]{2,1,0:T(8,128)S(1)} %get-tuple-element.37., ...), custom_call_target="tpu_custom_call" | custom-call | tf_op jit(solution)/shard_map/pallas_call | solution.py:394
  16.3 0.3 collective-permute-done.4.far_strip
  16.6 1.8 %collective-permute-done.5.near_strip = f32[4,8,128]{2,1,0:T(8,128)S(1)} collective-permute-done((f32[4,8,128]{2,1,0:T(8,128)S(1)}, f32[4,8,128]{2,1,0:T(8,128)S(1)}, u32[]{:S(2)}, u32[]{:S(2)}) %collective-permute-start.5) | collective-permute-done | bytes 16416 | tf_op jit(solution)/shard_map/ppermute | solution.py:415
  18.4 0.9 %shard_map.62 = (f32[256,128]{1,0:T(8,128)S(1)}, f32[16,16,128]{2,1,0:T(8,128)S(1)}, f32[16,16,128]{2,1,0:T(8,128)S(1)}, f32[16,16,128]{2,1,0:T(8,128)S(1)}, f32...) custom-call(f32[16,16,128]{2,1,0:T(8,128)S(1)} %get-tuple-element.43, ...), custom_call_target="tpu_custom_call" | custom-call | tf_op jit(solution)/shard_map/pallas_call | solution.py:394
  19.3 24.1 %all_to_all.11 = f32[256,1,128]{2,1,0:T(1,128)S(1)} all-to-all(f32[256,1,128]{2,1,0:T(1,128)S(1)} %bitcast.10), channel_id=1, replica_groups=mesh['gx'=16,'gy'=16] {'gx','gy'}, dimensions={0} | all-to-all | bytes 262144 | tf_op jit(solution)/shard_map/all_to_all | solution.py:449
  43.4 1.2 %finish.1 = (f32[16,8,128]{2,1,0:T(8,128)}, f32[16,8,128]{2,1,0:T(8,128)}) custom-call(f32[256,128]{1,0:T(8,128)S(1)} %bitcast.9, f32[16,8,128]{2,1,0:T(8,128)S(1)} %get-tuple-element.39.p.p_own, f32[16,16,128]{2,1,0:T(8,128)S(1)} %get-tuple-element.55.z0, f32[16,16,128]{2,1,0:T(8,128)S(1)} %get-tuple-element.56.v, f32[16,16,128]{2,1,0:T(8,128)S(1)} %get-tuple-element.57.s, ...), custom_call_target="tpu_custom_call" | custom-call | tf_op jit(solution)/shard_map/finish/pallas_call | solution.py:451
  (1 shorter events, 0.0 us)
Async XLA Ops:
  1.8 13.9 %collective-permute-start = (f32[32,8,128]{2,1,0:T(8,128)S(1)}, f32[32,8,128]{2,1,0:T(8,128)S(1)}, u32[]{:S(2)}, u32[]{:S(2)}) collective-permute-start(f32[32,8,128]{2,1,0:T(8,128)S(1)} %get-tuple-element.41), channel_id=1, source_target_pairs={{0,1},{1,0},{2,3},{3,2},{4,5},{5,4},{6,7},{7,6},{8,9},{9,8},{10,11... | collective-permute-start | bytes 393224 | tf_op jit(solution)/shard_map/ppermute | solution.py:415
  5.1 10.7 %collective-permute-start.1 = (f32[32,8,128]{2,1,0:T(8,128)S(1)}, f32[32,8,128]{2,1,0:T(8,128)S(1)}, u32[]{:S(2)}, u32[]{:S(2)}) collective-permute-start(f32[32,8,128]{2,1,0:T(8,128)S(1)} %get-tuple-element.42), channel_id=1, source_target_pairs={{0,16},{1,17},{2,18},{3,19},{4,20},{5,21},{6,22},{7,23},{8,24},{9,... | collective-permute-start | bytes 393224 | tf_op jit(solution)/shard_map/ppermute | solution.py:415
  5.3 4.4 %collective-permute-start.3 = (f32[2,8,128]{2,1,0:T(8,128)S(1)}, f32[2,8,128]{2,1,0:T(8,128)S(1)}, u32[]{:S(2)}, u32[]{:S(2)}) collective-permute-start(f32[2,8,128]{2,1,0:T(8,128)S(1)} %get-tuple-element.49.own_first), channel_id=1, source_target_pairs={{0,15},{1,0},{2,1},{3,2},{4,3},{5,4},{6,5},{7,6},{8,7},{9,8},{10,9... | collective-permute-start | bytes 24584 | tf_op jit(solution)/shard_map/ppermute | solution.py:406
  6.6 5.4 %collective-permute-start.2 = (f32[2,8,128]{2,1,0:T(8,128)S(1)}, f32[2,8,128]{2,1,0:T(8,128)S(1)}, u32[]{:S(2)}, u32[]{:S(2)}) collective-permute-start(f32[2,8,128]{2,1,0:T(8,128)S(1)} %get-tuple-element.50.own_last), channel_id=1, source_target_pairs={{0,1},{1,2},{2,3},{3,4},{4,5},{5,6},{6,7},{7,8},{8,9},{9,10},{10,1... | collective-permute-start | bytes 24584 | tf_op jit(solution)/shard_map/ppermute | solution.py:406
  12.1 4.5 %collective-permute-start.4 = (f32[4,8,128]{2,1,0:T(8,128)S(1)}, f32[4,8,128]{2,1,0:T(8,128)S(1)}, u32[]{:S(2)}, u32[]{:S(2)}) collective-permute-start(f32[4,8,128]{2,1,0:T(8,128)S(1)} %get-tuple-element.52), channel_id=1, source_target_pairs={{0,1},{1,0},{2,3},{3,2},{4,5},{5,4},{6,7},{7,6},{8,9},{9,8},{10,11... | collective-permute-start | bytes 49160 | tf_op jit(solution)/shard_map/ppermute | solution.py:415
  15.8 2.6 %collective-permute-start.5 = (f32[4,8,128]{2,1,0:T(8,128)S(1)}, f32[4,8,128]{2,1,0:T(8,128)S(1)}, u32[]{:S(2)}, u32[]{:S(2)}) collective-permute-start(f32[4,8,128]{2,1,0:T(8,128)S(1)} %get-tuple-element.53), channel_id=1, source_target_pairs={{0,16},{1,17},{2,18},{3,19},{4,20},{5,21},{6,22},{7,23},{8,24},{9,... | collective-permute-start | bytes 49160 | tf_op jit(solution)/shard_map/ppermute | solution.py:415

commit v3 on v2

--- a/solution.py
+++ b/solution.py
@@ -315,7 +315,10 @@
 
 def finish(sums, p_own, z0, v, s, q, f0, fpx, fpy, fpz, fz, fv, s_pack, q_pack, fp_pack, fz_pack, fv_pack,
            pressure_out, s_out, flow, f1, s1, wy0_ends, wy1_ends, pressure, s_new, sems):
-    total = jnp.sum(sums[...], axis=0, keepdims=True)
+    parts = [sums[i:i + ROWS] for i in range(0, sums.shape[0], ROWS)]
+    while len(parts) > 1:
+        parts = [sum(parts[i + 1:i + 2], parts[i]) for i in range(0, len(parts), 2)]
+    total = jnp.sum(parts[0], axis=0, keepdims=True)
     lane = lanes((1, LANES))
     rz, zaz, rv, vaz, vav = (jnp.sum(jnp.where(lane == i, total, 0.0), axis=1, keepdims=True) for i in range(5))
     ratio = vaz / zaz

time: 44.8 us -> 44.8 us (level)
  no operation moved by 1% of the time
where the time goes in v3:
time: 44.8 us; the launch traced here: 44.6 us
  blocking collectives  24.1 us (54%)
  starting transfers between devices  9.97 us (22%)
  waiting for transfers between devices  5.95 us (13%)
  Pallas kernels  3.86 us (9%)
  between operations  0.68 us (2%)
    all_to_all x1, blocking collectives, one_sample(): sums = lax.all_to_all(sums, ('gx', 'gy'), 0, 0, tiled=True)  24.1 us
    ppermute x4, starting transfers between devices, trade(): return lax.ppermute(x, ('gx', 'gy'), pairs)  7.21 us
    ppermute x2, waiting for transfers between devices, ring(): return lax.ppermute(x, axis, [(i, (i + by) % n) for i in range(n)])  3.87 us
    ppermute x2, starting transfers between devices, ring(): return lax.ppermute(x, axis, [(i, (i + by) % n) for i in range(n)])  2.76 us
    ppermute x4, waiting for transfers between devices, trade(): return lax.ppermute(x, ('gx', 'gy'), pairs)  2.07 us
    pallas_call x4, Pallas kernels, call(): pl.pallas_call(body, compiler_params=SCRATCH, out_shape=tuple((pltpu.VMEM...  1.52 us
    pallas_call x1, Pallas kernels, one_sample(): pl.pallas_call(finish, name='finish', compiler_params=SCRATCH, out_shape=...  1.18 us
    pallas_call x1, Pallas kernels, one_sample(): pl.pallas_call(pack_columns, name='pack_columns', compiler_params=SCRATCH...  1.15 us
  transfers between devices with their start and end apart: 6, of which 4 were waited for; matrix products, arithmetic and copies ran while one was open for 0% of the time, Pallas kernels for 1%

profile of v3, /device:TPU:1, one launch (start us, length us, event | category | flops | bytes accessed | tf_op | source)
XLA Modules:
  0.0 44.6 jit_solution(9483662055198509599)
XLA Ops:
  0.6 1.2 %pack_columns.1 = (f32[2,8,128]{2,1,0:T(8,128)S(1)}, f32[2,8,128]{2,1,0:T(8,128)S(1)}, f32[16,8,128]{2,1,0:T(8,128)S(1)}, f32[16,8,128]{2,1,0:T(8,128)S(1)}, f32...) custom-call(f32[16,8,128]{2,1,0:T(8,128)} %bitcast.11, f32[16,8,128]{2,1,0:T(8,128)} %bitcast.12, ...), custom_call_target="tpu_custom_call" | custom-call | tf_op jit(solution)/shard_map/pack_columns/pallas_call | solution.py:425
  1.8 3.3 %collective-permute-start = (f32[32,8,128]{2,1,0:T(8,128)S(1)}, f32[32,8,128]{2,1,0:T(8,128)S(1)}, u32[]{:S(2)}, u32[]{:S(2)}) collective-permute-start(f32[32,8,128]{2,1,0:T(8,128)S(1)} %get-tuple-element.41), channel_id=1, source_target_pairs={{0,1},{1,0},{2,3},{3,2},{4,5},{5,4},{6,7},{7,6},{8,9},{9,8},{10,11... | collective-permute-start | bytes 393224 | tf_op jit(solution)/shard_map/ppermute | solution.py:418
  5.1 0.2 collective-permute-start.1
  5.3 1.2 %collective-permute-start.3 = (f32[2,8,128]{2,1,0:T(8,128)S(1)}, f32[2,8,128]{2,1,0:T(8,128)S(1)}, u32[]{:S(2)}, u32[]{:S(2)}) collective-permute-start(f32[2,8,128]{2,1,0:T(8,128)S(1)} %get-tuple-element.49.own_first), channel_id=1, source_target_pairs={{0,15},{1,0},{2,1},{3,2},{4,3},{5,4},{6,5},{7,6},{8,7},{9,8},{10,9... | collective-permute-start | bytes 24584 | tf_op jit(solution)/shard_map/ppermute | solution.py:409
  6.6 1.5 %collective-permute-start.2 = (f32[2,8,128]{2,1,0:T(8,128)S(1)}, f32[2,8,128]{2,1,0:T(8,128)S(1)}, u32[]{:S(2)}, u32[]{:S(2)}) collective-permute-start(f32[2,8,128]{2,1,0:T(8,128)S(1)} %get-tuple-element.50.own_last), channel_id=1, source_target_pairs={{0,1},{1,2},{2,3},{3,4},{4,5},{5,6},{6,7},{7,8},{8,9},{9,10},{10,1... | collective-permute-start | bytes 24584 | tf_op jit(solution)/shard_map/ppermute | solution.py:409
  8.1 1.6 %collective-permute-done.3.from_next = f32[2,8,128]{2,1,0:T(8,128)S(1)} collective-permute-done((f32[2,8,128]{2,1,0:T(8,128)S(1)}, f32[2,8,128]{2,1,0:T(8,128)S(1)}, u32[]{:S(2)}, u32[]{:S(2)}) %collective-permute-start.3) | collective-permute-done | bytes 8224 | tf_op jit(solution)/shard_map/ppermute | solution.py:409
  9.7 2.2 %collective-permute-done.2.from_prev = f32[2,8,128]{2,1,0:T(8,128)S(1)} collective-permute-done((f32[2,8,128]{2,1,0:T(8,128)S(1)}, f32[2,8,128]{2,1,0:T(8,128)S(1)}, u32[]{:S(2)}, u32[]{:S(2)}) %collective-permute-start.2) | collective-permute-done | bytes 8224 | tf_op jit(solution)/shard_map/ppermute | solution.py:409
  12.0 0.1 shard_map.61
  12.1 3.7 %collective-permute-start.4 = (f32[4,8,128]{2,1,0:T(8,128)S(1)}, f32[4,8,128]{2,1,0:T(8,128)S(1)}, u32[]{:S(2)}, u32[]{:S(2)}) collective-permute-start(f32[4,8,128]{2,1,0:T(8,128)S(1)} %get-tuple-element.52), channel_id=1, source_target_pairs={{0,1},{1,0},{2,3},{3,2},{4,5},{5,4},{6,7},{7,6},{8,9},{9,8},{10,11... | collective-permute-start | bytes 49160 | tf_op jit(solution)/shard_map/ppermute | solution.py:418
  15.8 0.0 collective-permute-start.5
  15.8 0.0 collective-permute-done.far
  15.8 0.0 collective-permute-done.1.near
  15.8 0.5 %shard_map.60 = (f32[16,16,128]{2,1,0:T(8,128)S(1)}, f32[16,16,128]{2,1,0:T(8,128)S(1)}, f32[16,16,128]{2,1,0:T(8,128)S(1)}, f32[16,16,128]{2,1,0:T(8,128)S(1)},...) custom-call(f32[16,8,128]{2,1,0:T(8,128)S(1)} %get-tuple-element.37., ...), custom_call_target="tpu_custom_call" | custom-call | tf_op jit(solution)/shard_map/pallas_call | solution.py:397
  16.3 0.3 collective-permute-done.4.far_strip
  16.6 1.8 %collective-permute-done.5.near_strip = f32[4,8,128]{2,1,0:T(8,128)S(1)} collective-permute-done((f32[4,8,128]{2,1,0:T(8,128)S(1)}, f32[4,8,128]{2,1,0:T(8,128)S(1)}, u32[]{:S(2)}, u32[]{:S(2)}) %collective-permute-start.5) | collective-permute-done | bytes 16416 | tf_op jit(solution)/shard_map/ppermute | solution.py:418
  18.4 0.9 %shard_map.62 = (f32[256,128]{1,0:T(8,128)S(1)}, f32[16,16,128]{2,1,0:T(8,128)S(1)}, f32[16,16,128]{2,1,0:T(8,128)S(1)}, f32[16,16,128]{2,1,0:T(8,128)S(1)}, f32...) custom-call(f32[16,16,128]{2,1,0:T(8,128)S(1)} %get-tuple-element.43, ...), custom_call_target="tpu_custom_call" | custom-call | tf_op jit(solution)/shard_map/pallas_call | solution.py:397
  19.3 24.1 %all_to_all.11 = f32[256,1,128]{2,1,0:T(1,128)S(1)} all-to-all(f32[256,1,128]{2,1,0:T(1,128)S(1)} %bitcast.10), channel_id=1, replica_groups=mesh['gx'=16,'gy'=16] {'gx','gy'}, dimensions={0} | all-to-all | bytes 262144 | tf_op jit(solution)/shard_map/all_to_all | solution.py:452
  43.4 1.2 %finish.1 = (f32[16,8,128]{2,1,0:T(8,128)}, f32[16,8,128]{2,1,0:T(8,128)}) custom-call(f32[256,128]{1,0:T(8,128)S(1)} %bitcast.9, f32[16,8,128]{2,1,0:T(8,128)S(1)} %get-tuple-element.39.p.p_own, f32[16,16,128]{2,1,0:T(8,128)S(1)} %get-tuple-element.55.z0, f32[16,16,128]{2,1,0:T(8,128)S(1)} %get-tuple-element.56.v, f32[16,16,128]{2,1,0:T(8,128)S(1)} %get-tuple-element.57.s, ...), custom_call_target="tpu_custom_call" | custom-call | tf_op jit(solution)/shard_map/finish/pallas_call | solution.py:454
  (1 shorter events, 0.0 us)
Async XLA Ops:
  1.8 13.9 %collective-permute-start = (f32[32,8,128]{2,1,0:T(8,128)S(1)}, f32[32,8,128]{2,1,0:T(8,128)S(1)}, u32[]{:S(2)}, u32[]{:S(2)}) collective-permute-start(f32[32,8,128]{2,1,0:T(8,128)S(1)} %get-tuple-element.41), channel_id=1, source_target_pairs={{0,1},{1,0},{2,3},{3,2},{4,5},{5,4},{6,7},{7,6},{8,9},{9,8},{10,11... | collective-permute-start | bytes 393224 | tf_op jit(solution)/shard_map/ppermute | solution.py:418
  5.1 10.7 %collective-permute-start.1 = (f32[32,8,128]{2,1,0:T(8,128)S(1)}, f32[32,8,128]{2,1,0:T(8,128)S(1)}, u32[]{:S(2)}, u32[]{:S(2)}) collective-permute-start(f32[32,8,128]{2,1,0:T(8,128)S(1)} %get-tuple-element.42), channel_id=1, source_target_pairs={{0,16},{1,17},{2,18},{3,19},{4,20},{5,21},{6,22},{7,23},{8,24},{9,... | collective-permute-start | bytes 393224 | tf_op jit(solution)/shard_map/ppermute | solution.py:418
  5.3 4.4 %collective-permute-start.3 = (f32[2,8,128]{2,1,0:T(8,128)S(1)}, f32[2,8,128]{2,1,0:T(8,128)S(1)}, u32[]{:S(2)}, u32[]{:S(2)}) collective-permute-start(f32[2,8,128]{2,1,0:T(8,128)S(1)} %get-tuple-element.49.own_first), channel_id=1, source_target_pairs={{0,15},{1,0},{2,1},{3,2},{4,3},{5,4},{6,5},{7,6},{8,7},{9,8},{10,9... | collective-permute-start | bytes 24584 | tf_op jit(solution)/shard_map/ppermute | solution.py:409
  6.6 5.4 %collective-permute-start.2 = (f32[2,8,128]{2,1,0:T(8,128)S(1)}, f32[2,8,128]{2,1,0:T(8,128)S(1)}, u32[]{:S(2)}, u32[]{:S(2)}) collective-permute-start(f32[2,8,128]{2,1,0:T(8,128)S(1)} %get-tuple-element.50.own_last), channel_id=1, source_target_pairs={{0,1},{1,2},{2,3},{3,4},{4,5},{5,6},{6,7},{7,8},{8,9},{9,10},{10,1... | collective-permute-start | bytes 24584 | tf_op jit(solution)/shard_map/ppermute | solution.py:409
  12.1 4.5 %collective-permute-start.4 = (f32[4,8,128]{2,1,0:T(8,128)S(1)}, f32[4,8,128]{2,1,0:T(8,128)S(1)}, u32[]{:S(2)}, u32[]{:S(2)}) collective-permute-start(f32[4,8,128]{2,1,0:T(8,128)S(1)} %get-tuple-element.52), channel_id=1, source_target_pairs={{0,1},{1,0},{2,3},{3,2},{4,5},{5,4},{6,7},{7,6},{8,9},{9,8},{10,11... | collective-permute-start | bytes 49160 | tf_op jit(solution)/shard_map/ppermute | solution.py:418
  15.8 2.6 %collective-permute-start.5 = (f32[4,8,128]{2,1,0:T(8,128)S(1)}, f32[4,8,128]{2,1,0:T(8,128)S(1)}, u32[]{:S(2)}, u32[]{:S(2)}) collective-permute-start(f32[4,8,128]{2,1,0:T(8,128)S(1)} %get-tuple-element.53), channel_id=1, source_target_pairs={{0,16},{1,17},{2,18},{3,19},{4,20},{5,21},{6,22},{7,23},{8,24},{9,... | collective-permute-start | bytes 49160 | tf_op jit(solution)/shard_map/ppermute | solution.py:418
